TPU v7x, 128 devices: a whole 4x4x4 slice. The times are simulated.
128 devices in a mesh: gx: 8 (over z, core), gy: 4 (over x), gz: 4 (over y).
Axes of the slice: x: 4, y: 4, z: 4, core: 2. Of those that a mesh axis runs over, the one named last changes fastest.
Arguments:
- snapshots: float32 [16, 128, 128, 1024], P(None, 'gx', 'gy', 'gz'), as said below
- diffusivity: float32 [128, 128, 1024], P('gx', 'gy', 'gz'), may hold values from 0.02 to 0.16
Outputs:
- shifted: float32 [16, 128, 128, 1024], P(None, 'gx', 'gy', 'gz')
- reduced: float32 [16, 16], replicated
- sigmas: float32 [16], replicated
Inputs may be any that keep to these rules, and one draw needn't show every extreme that they name: `snapshots`: real values.
All inputs are finite; a program needn't handle non-finite values.
Results may differ from a plain program's by a relative error of at most 0.0003.
Values sent between devices are 32-bit elements; how exact they have to be, the bound alone decides.
A program may use at most 128 MiB of HBM per device.

v0:
```python
import jax
import jax.numpy as jnp
import numpy as np
from jax import lax
from jax.sharding import PartitionSpec as P

SNAPS = 16
RANK = 12
SWEEPS = 6


def extended(block, sides, width):
    for axis, dim in sides:
        count = lax.axis_size(axis)
        forward = [(i, i + 1) for i in range(count - 1)]
        forward.append((count - 1, 0))
        backward = [(target, source) for source, target in forward]
        low = lax.ppermute(
            lax.slice_in_dim(block, block.shape[dim] - width, None, axis=dim), axis, forward
        )
        high = lax.ppermute(lax.slice_in_dim(block, 0, width, axis=dim), axis, backward)
        block = jnp.concatenate([low, block, high], axis=dim)
    return block


def round_pairs(count):
    players = list(range(count))
    firsts = []
    seconds = []
    for turn in range(count - 1):
        firsts.append([players[i] for i in range(count // 2)])
        seconds.append([players[count - 1 - i] for i in range(count // 2)])
        players = [players[0]] + [players[-1]] + players[1:-1]
    return (np.array(firsts, dtype=np.int32), np.array(seconds, dtype=np.int32))


def jacobi_eigen(small):
    count = small.shape[0]
    first_np, second_np = round_pairs(count)
    firsts = jnp.asarray(first_np)
    seconds = jnp.asarray(second_np)
    eye = jnp.eye(count, dtype=jnp.float32)
    high = lax.Precision.HIGHEST

    def turn(step, carry):
        mat, vecs = carry
        row = step % (count - 1)
        pidx = firsts[row]
        qidx = seconds[row]
        app = mat[pidx, pidx]
        aqq = mat[qidx, qidx]
        apq = mat[pidx, qidx]
        tau = aqq - app
        sgn = jnp.where(tau >= 0, 1.0, -1.0).astype(jnp.float32)
        denom = jnp.abs(tau) + jnp.sqrt(tau * tau + 4.0 * apq * apq)
        tangent = jnp.where(denom > 0, 2.0 * apq * sgn / jnp.where(denom > 0, denom, 1.0), 0.0)
        cosine = 1.0 / jnp.sqrt(1.0 + tangent * tangent)
        sine = tangent * cosine
        onep = jax.nn.one_hot(pidx, count, dtype=jnp.float32)
        oneq = jax.nn.one_hot(qidx, count, dtype=jnp.float32)
        rot = eye + jnp.dot(onep.T, (cosine - 1.0)[:, None] * onep, precision=high)
        rot = rot + jnp.dot(oneq.T, (cosine - 1.0)[:, None] * oneq, precision=high)
        rot = rot + jnp.dot(onep.T, sine[:, None] * oneq, precision=high)
        rot = rot - jnp.dot(oneq.T, sine[:, None] * onep, precision=high)
        mat = jnp.dot(jnp.dot(rot.T, mat, precision=high), rot, precision=high)
        vecs = jnp.dot(vecs, rot, precision=high)
        return (mat, vecs)

    mat, vecs = lax.fori_loop(0, SWEEPS * (count - 1), turn, (small, eye))
    return (jnp.diagonal(mat), vecs)


def factor_pair(gram, cross):
    lower = jnp.linalg.cholesky(gram)
    proj = lax.linalg.triangular_solve(lower, cross, left_side=True, lower=True)
    return (lower.T, proj)


def finish(upper, proj, ncell):
    high = lax.Precision.HIGHEST
    small = jnp.dot(upper, upper.T, precision=high) / ncell
    lam, vecs = jacobi_eigen(small)
    ordered = jnp.sort(lam)[::-1]
    sigmas = jnp.sqrt(ordered)
    keep = (lam >= ordered[RANK - 1]).astype(jnp.float32)
    projector = jnp.dot(vecs * keep[None, :], vecs.T, precision=high)
    inverse = jnp.dot(vecs * (keep / lam)[None, :], vecs.T, precision=high) / ncell
    reduced = jnp.dot(jnp.dot(projector, proj, precision=high), upper.T, precision=high)
    reduced = jnp.dot(reduced, inverse, precision=high)
    return (reduced, sigmas)


def view(padded, dim, offset):
    leading = tuple((slice(None) for lead_pos in range(padded.ndim - 3)))
    parts = [slice(2, padded.shape[padded.ndim - 3 + axis_pos] - 2) for axis_pos in range(3)]
    length = padded.shape[padded.ndim - 3 + dim] - 4
    parts[dim] = slice(2 + offset, 2 + offset + length)
    return padded[leading + tuple(parts)]


def advance(padded, diffusivity):
    field = view(padded, 0, 0)
    lap = -6.0 * field
    for dim in range(3):
        lap = lap + view(padded, dim, 1) + view(padded, dim, -1)

    def slope(dim):
        return (
            8.0 * (view(padded, dim, 1) - view(padded, dim, -1))
            - (view(padded, dim, 2) - view(padded, dim, -2))
        ) / 12.0

    return (
        field
        + diffusivity * lap
        - (0.3 + 0.02 * field) * slope(2)
        - 0.2 * slope(0)
        - 0.15 * slope(1)
    )


def shards(snapshots, diffusivity):
    high = lax.Precision.HIGHEST

    def one_field(index, collected):
        field = lax.dynamic_index_in_dim(snapshots, index, 0, keepdims=False)
        padded = extended(field, (("gx", 0), ("gy", 1), ("gz", 2)), 2)
        return lax.dynamic_update_index_in_dim(collected, advance(padded, diffusivity), index, 0)

    shifted = lax.fori_loop(0, snapshots.shape[0], one_field, jnp.zeros_like(snapshots))
    flat_x = snapshots.reshape(SNAPS, -1)
    flat_y = shifted.reshape(SNAPS, -1)
    gram = jnp.dot(flat_x, flat_x.T, precision=high)
    cross = jnp.dot(flat_x, flat_y.T, precision=high)
    ncell = float(flat_x.shape[1] * lax.axis_size("gx") * lax.axis_size("gy") * lax.axis_size("gz"))
    gram, cross = lax.psum((gram, cross), ("gx", "gy", "gz"))
    upper, proj = factor_pair(gram, cross)
    reduced, sigmas = finish(upper, proj, ncell)
    return (shifted, reduced, sigmas)


def solution(mesh):
    placed = (P(None, "gx", "gy", "gz"), P("gx", "gy", "gz"))
    return jax.shard_map(
        shards,
        mesh=mesh,
        in_specs=placed,
        out_specs=(P(None, "gx", "gy", "gz"), P(), P()),
        check_vma=False,
    )
```

profile of v0, /device:TPU:1, one launch (start us, length us, event | category | flops | bytes accessed | tf_op | source)
XLA Modules:
  0.0 981.1 jit_solution(14451856743499966787)
XLA Ops:
  0.6 407.2 %while.34 = (s32[]{:T(128)}, f32[16,16,32,256]{3,2,1,0:T(8,128)}, f32[16,16,32,256]{3,2,1,0:T(8,128)}, f32[16,32,256]{2,1,0:T(8,128)}, s32[]{:T(128)}, /*index=5*/s32[]{:T(128)}, s32[]{}) while((s32[]{:T(128)}, f32[16,16,32,256]{3,2,1,0:T(8,128)}, f32[16,16,32,256]{3,2,1,0:T(8,128)}, f32[16,32,256]{2,1,0:T(8,128)}, s32[]{:T(128)}, ...), condition=%wide.region_1.2_spmd, body=%wide.region_0.1_spmd.sunk | while | flops 8900611 | bytes 10468449 | solution.py:130
  7.3 2.5 collective-permute-start.2
  11.0 3.0 collective-permute-done.3
  17.2 5.1 collective-permute-done.4
  22.4 3.8 fusion.118
  27.0 7.0 collective-permute-start
  43.8 5.2 collective-permute-done.4
  49.0 3.8 fusion.118
  53.6 6.8 collective-permute-start
  67.3 2.0 collective-permute-start.5
  69.5 5.1 collective-permute-done.4
  74.6 3.8 fusion.118
  79.2 6.3 collective-permute-start
  93.8 1.8 collective-permute-start.5
  95.7 6.0 collective-permute-done.4
  101.7 3.8 fusion.118
  106.3 4.2 collective-permute-start
  121.5 6.5 collective-permute-done.4
  128.0 3.8 fusion.118
  132.6 3.7 collective-permute-start
  145.0 1.8 collective-permute-start.5
  146.9 6.2 collective-permute-done.4
  153.2 3.8 fusion.118
  157.8 4.0 collective-permute-start
  170.2 1.8 collective-permute-start.5
  172.2 6.1 collective-permute-done.4
  178.3 3.8 fusion.118
  182.9 4.1 collective-permute-start
  194.4 1.8 collective-permute-start.5
  196.3 5.1 collective-permute-done.4
  201.4 3.8 fusion.118
  206.1 5.8 collective-permute-start
  220.4 1.8 collective-permute-start.5
  222.3 6.2 collective-permute-done.4
  228.5 3.8 fusion.118
  233.1 4.0 collective-permute-start
  248.1 6.5 collective-permute-done.4
  254.6 3.8 fusion.118
  259.2 3.7 collective-permute-start
  273.4 6.1 collective-permute-done.4
  279.5 3.8 fusion.118
  284.1 4.1 collective-permute-start
  295.8 1.8 collective-permute-start.5
  297.8 5.1 collective-permute-done.4
  302.9 3.8 fusion.118
  307.6 5.5 collective-permute-start
  321.5 1.8 collective-permute-start.5
  323.5 6.0 collective-permute-done.4
  329.5 3.8 fusion.118
  334.2 4.2 collective-permute-start
  347.3 1.8 collective-permute-start.5
  349.2 6.5 collective-permute-done.4
  355.8 3.8 fusion.118
  360.4 3.7 collective-permute-start
  374.6 6.1 collective-permute-done.4
  380.7 3.8 fusion.118
  385.3 4.1 collective-permute-start
  396.9 1.8 collective-permute-start.5
  398.9 5.1 collective-permute-done.4
  404.0 3.8 fusion.118
  407.8 25.4 %fusion.56 = f32[16,16]{0,1:T(8,128)S(1)} fusion(f32[16,16,32,256]{3,2,1,0:T(8,128)} %get-tuple-element.458, f32[16,16,32,256]{3,2,1,0:T(8,128)} %get-tuple-element.270), kind=kOutput, calls=%fused_computation.108 | convolution fusion | flops 402653184 | bytes 16778240 | tf_op jit(solution)/shard_map/dot_general | solution.py:134
  433.2 14.0 %fusion.53 = f32[16,16]{0,1:T(8,128)S(1)} fusion(f32[16,16,32,256]{3,2,1,0:T(8,128)S(1)} %copy-done), kind=kOutput, calls=%fused_computation.105 | convolution fusion | flops 402653184 | bytes 8389632 | tf_op jit(solution)/shard_map/dot_general | solution.py:133
  447.2 69.8 %all-reduce = (f32[16,16]{0,1:T(8,128)S(1)}, f32[16,16]{0,1:T(8,128)S(1)}) all-reduce(f32[16,16]{0,1:T(8,128)S(1)} %fusion.53, f32[16,16]{0,1:T(8,128)S(1)} %fusion.56), channel_id=1, replica_groups=mesh['gx'=8,'gy'=4,'gz'=4] {'gx','gy','gz'}, use_global_device_ids=true, to_apply=%region_2.3 | all-reduce | flops 512 | bytes 4096 | tf_op jit(solution)/shard_map/psum | solution.py:136
  520.2 452.1 %while.35 = (s32[]{:T(128)}, f32[16,16]{1,0:T(8,128)S(1)}, f32[16,16]{0,1:T(8,128)S(1)}, s32[]{:T(128)}, s32[15,8]{1,0:T(8,128)}, /*index=5*/s32[]{:T(128)}, s32[]{:T(128)}, s32[15,8]{1,0:T(8,128)}) while((s32[]{:T(128)}, f32[16,16]{1,0:T(8,128)S(1)}, f32[16,16]{0,1:T(8,128)S(1)}, s32[]{:T(128)}, ...), condition=%wide.region_6.7_spmd.clone.clone, body=%wide.region_5.6_spmd.sunk.clone.clone.sunk | while | flops 249131 | bytes 19833 | solution.py:69
  (1623 shorter events, 620.6 us)
Async XLA Ops:
  1.5 5.0 collective-permute-start
  2.9 4.3 collective-permute-start.1
  9.9 4.1 collective-permute-start.3
  14.2 8.1 collective-permute-start.4
  15.6 6.8 collective-permute-start.5
  27.0 8.1 collective-permute-start
  36.5 4.1 collective-permute-start.3
  40.9 8.1 collective-permute-start.4
  41.9 7.0 collective-permute-start.5
  53.6 7.9 collective-permute-start
  61.8 4.1 collective-permute-start.3
  66.3 8.3 collective-permute-start.4
  67.3 7.3 collective-permute-start.5
  79.2 8.9 collective-permute-start
  88.3 4.1 collective-permute-start.3
  92.7 9.0 collective-permute-start.4
  93.8 7.9 collective-permute-start.5
  106.3 7.5 collective-permute-start
  114.0 4.1 collective-permute-start.3
  118.4 9.6 collective-permute-start.4
  119.5 8.5 collective-permute-start.5
  132.6 6.7 collective-permute-start
  139.5 4.1 collective-permute-start.3
  143.9 9.3 collective-permute-start.4
  145.0 8.2 collective-permute-start.5
  157.8 6.7 collective-permute-start
  164.8 4.1 collective-permute-start.3
  169.2 9.1 collective-permute-start.4
  170.2 8.0 collective-permute-start.5
  182.9 5.8 collective-permute-start
  188.9 4.1 collective-permute-start.3
  193.3 8.2 collective-permute-start.4
  194.4 7.1 collective-permute-start.5
  206.1 8.7 collective-permute-start
  214.8 4.1 collective-permute-start.3
  219.3 9.2 collective-permute-start.4
  220.4 8.1 collective-permute-start.5
  233.1 7.4 collective-permute-start
  240.6 4.1 collective-permute-start.3
  245.0 9.6 collective-permute-start.4
  246.1 8.5 collective-permute-start.5
  259.2 6.6 collective-permute-start
  266.0 4.1 collective-permute-start.3
  270.3 9.2 collective-permute-start.4
  271.4 8.1 collective-permute-start.5
  284.1 6.2 collective-permute-start
  290.4 4.1 collective-permute-start.3
  294.8 8.1 collective-permute-start.4
  295.8 7.1 collective-permute-start.5
  307.6 8.3 collective-permute-start
  316.0 4.1 collective-permute-start.3
  320.5 9.1 collective-permute-start.4
  321.5 8.0 collective-permute-start.5
  334.2 7.5 collective-permute-start
  341.8 4.1 collective-permute-start.3
  346.2 9.6 collective-permute-start.4
  347.3 8.5 collective-permute-start.5
  360.4 6.6 collective-permute-start
  371.5 9.2 collective-permute-start.4
  372.6 8.1 collective-permute-start.5
  385.3 6.1 collective-permute-start
  391.5 4.1 collective-permute-start.3
  396.0 8.1 collective-permute-start.4
  396.9 7.1 collective-permute-start.5
  (33 other events, 116.5 us)
where the time goes:
time: 993 us; the launch traced here: 981 us
  local copies, waits for them, and re-layouts  275 us (28%)
  matrix products  186 us (19%)
  starting transfers between devices  157 us (16%)
  waiting for transfers between devices  151 us (15%)
  other arithmetic  139 us (14%)
  blocking collectives  69.8 us (7%)
    ppermute x48, waiting for transfers between devices, extended(): lax.ppermute(lax.slice_in_dim(block, block.shape[dim] - width, None, axis...  117 us
    ppermute x48, starting transfers between devices, extended(): lax.ppermute(lax.slice_in_dim(block, 0, width, axis=dim), axis, backward)  106 us
    psum x1, blocking collectives, shards(): gram, cross = lax.psum((gram, cross), ('gx', 'gy', 'gz'))  69.8 us
    concatenate x90, other arithmetic, turn(): app = mat[pidx, pidx]  65.6 us
    eq x90, local copies, waits for them, and re-layouts, turn(): onep = jax.nn.one_hot(pidx, count, dtype=jnp.float32)  64.9 us
    dynamic_update_slice x16, other arithmetic, one_field(): lax.dynamic_update_index_in_dim(collected, advance(padded, diffusivity),...  60 us
    gather x90, local copies, waits for them, and re-layouts, turn(): aqq = mat[qidx, qidx]  58.1 us
    gather x90, local copies, waits for them, and re-layouts, turn(): app = mat[pidx, pidx]  58.1 us
  transfers between devices with their start and end apart: 96, of which 65 were waited for; matrix products, arithmetic and copies ran while one was open for 2% of the time, Pallas kernels for 0%

commit v1 on v0

--- a/solution.py
+++ b/solution.py
@@ -3,6 +3,7 @@
 import numpy as np
 from jax import lax
 from jax.sharding import PartitionSpec as P
+from jax.lax import psum
 
 SNAPS = 16
 RANK = 12
@@ -133,7 +134,7 @@
     gram = jnp.dot(flat_x, flat_x.T, precision=high)
     cross = jnp.dot(flat_x, flat_y.T, precision=high)
     ncell = float(flat_x.shape[1] * lax.axis_size("gx") * lax.axis_size("gy") * lax.axis_size("gz"))
-    gram, cross = lax.psum((gram, cross), ("gx", "gy", "gz"))
+    gram, cross = psum(psum((gram, cross), axis_name="gx"), axis_name=("gy", "gz"))
     upper, proj = factor_pair(gram, cross)
     reduced, sigmas = finish(upper, proj, ncell)
     return (shifted, reduced, sigmas)

time: 993 us -> 1020 us (1.027)
  the two profiles are of different devices: /device:TPU:1 before, /device:TPU:0 now
where the time goes in v1:
time: 1020 us; the launch traced here: 1010 us
  local copies, waits for them, and re-layouts  275 us (27%)
  waiting for transfers between devices  213 us (21%)
  matrix products  186 us (18%)
  other arithmetic  139 us (14%)
  starting transfers between devices  99.3 us (10%)
  blocking collectives  95.8 us (9%)
    ppermute x48, waiting for transfers between devices, extended(): lax.ppermute(lax.slice_in_dim(block, block.shape[dim] - width, None, axis...  175 us
    psum x1, blocking collectives, shards(): psum(psum((gram, cross), axis_name='gx'), axis_name=('gy', 'gz'))  72.3 us
    concatenate x90, other arithmetic, turn(): app = mat[pidx, pidx]  65.6 us
    eq x90, local copies, waits for them, and re-layouts, turn(): onep = jax.nn.one_hot(pidx, count, dtype=jnp.float32)  64.9 us
    dynamic_update_slice x16, other arithmetic, one_field(): lax.dynamic_update_index_in_dim(collected, advance(padded, diffusivity),...  60 us
    gather x90, local copies, waits for them, and re-layouts, turn(): aqq = mat[qidx, qidx]  58.1 us
    gather x90, local copies, waits for them, and re-layouts, turn(): app = mat[pidx, pidx]  58.1 us
    gather x90, local copies, waits for them, and re-layouts, turn(): apq = mat[pidx, qidx]  57.4 us
  transfers between devices with their start and end apart: 96, of which 84 were waited for; matrix products, arithmetic and copies ran while one was open for 2% of the time, Pallas kernels for 0%

profile of v1, /device:TPU:0, one launch (start us, length us, event | category | flops | bytes accessed | tf_op | source)
XLA Modules:
  0.0 1011.3 jit_solution(516598037169186359)
XLA Ops:
  0.6 411.3 %while.34 = (s32[]{:T(128)}, f32[16,16,32,256]{3,2,1,0:T(8,128)}, f32[16,16,32,256]{3,2,1,0:T(8,128)}, f32[16,32,256]{2,1,0:T(8,128)}, s32[]{:T(128)}, /*index=5*/s32[]{:T(128)}, s32[]{}) while((s32[]{:T(128)}, f32[16,16,32,256]{3,2,1,0:T(8,128)}, f32[16,16,32,256]{3,2,1,0:T(8,128)}, f32[16,32,256]{2,1,0:T(8,128)}, s32[]{:T(128)}, ...), condition=%wide.region_1.2_spmd, body=%wide.region_0.1_spmd.sunk | while | flops 8900611 | bytes 10468449 | solution.py:131
  1.5 3.6 collective-permute-start
  7.0 3.0 collective-permute-done.1
  10.1 2.8 collective-permute-start.2
  14.6 3.5 collective-permute-done.3
  21.8 5.8 collective-permute-done.4
  28.0 3.8 fusion.118
  35.8 3.0 collective-permute-done.1
  41.0 2.0 collective-permute-done.2
  46.4 2.0 collective-permute-start.5
  48.5 5.8 collective-permute-done.4
  54.4 3.8 fusion.118
  61.1 3.0 collective-permute-done.1
  71.0 2.6 collective-permute-start.5
  73.7 5.8 collective-permute-done.4
  79.5 3.8 fusion.118
  86.0 3.0 collective-permute-done.1
  89.2 2.0 collective-permute-start.3
  96.0 2.1 collective-permute-start.5
  98.2 6.3 collective-permute-done.4
  104.5 3.8 fusion.118
  111.1 3.0 collective-permute-done.1
  123.4 6.9 collective-permute-done.4
  130.3 3.8 fusion.118
  136.8 3.0 collective-permute-done.1
  149.1 6.6 collective-permute-done.4
  155.7 3.8 fusion.118
  162.3 3.0 collective-permute-done.1
  174.6 6.4 collective-permute-done.4
  181.0 3.8 fusion.118
  187.6 3.0 collective-permute-done.1
  200.0 5.8 collective-permute-done.4
  205.9 3.8 fusion.118
  212.4 3.0 collective-permute-done.1
  224.6 6.5 collective-permute-done.4
  231.1 3.8 fusion.118
  237.7 3.0 collective-permute-done.1
  242.8 2.0 collective-permute-done.2
  250.0 6.9 collective-permute-done.4
  256.9 3.8 fusion.118
  263.4 3.0 collective-permute-done.1
  275.7 6.5 collective-permute-done.4
  282.2 3.8 fusion.118
  288.8 3.0 collective-permute-done.1
  293.9 2.0 collective-permute-done.2
  301.1 5.8 collective-permute-done.4
  307.0 3.8 fusion.118
  313.6 3.0 collective-permute-done.1
  325.9 6.4 collective-permute-done.4
  332.3 3.8 fusion.118
  338.9 3.0 collective-permute-done.1
  351.1 6.9 collective-permute-done.4
  358.1 3.8 fusion.118
  364.6 3.0 collective-permute-done.1
  376.9 6.5 collective-permute-done.4
  383.4 3.8 fusion.118
  390.0 3.0 collective-permute-done.1
  402.3 5.8 collective-permute-done.4
  408.2 3.8 fusion.118
  411.9 25.4 %fusion.56 = f32[16,16]{0,1:T(8,128)S(1)} fusion(f32[16,16,32,256]{3,2,1,0:T(8,128)} %get-tuple-element.460, f32[16,16,32,256]{3,2,1,0:T(8,128)} %get-tuple-element.270), kind=kOutput, calls=%fused_computation.108 | convolution fusion | flops 402653184 | bytes 16778240 | tf_op jit(solution)/shard_map/dot_general | solution.py:135
  437.4 14.0 %fusion.53 = f32[16,16]{0,1:T(8,128)S(1)} fusion(f32[16,16,32,256]{3,2,1,0:T(8,128)S(1)} %copy-done), kind=kOutput, calls=%fused_computation.105 | convolution fusion | flops 402653184 | bytes 8389632 | tf_op jit(solution)/shard_map/dot_general | solution.py:134
  451.4 23.6 %all-reduce.1 = (f32[16,16]{0,1:T(8,128)S(1)}, f32[16,16]{0,1:T(8,128)S(1)}) all-reduce(f32[16,16]{0,1:T(8,128)S(1)} %fusion.53, f32[16,16]{0,1:T(8,128)S(1)} %fusion.56), channel_id=1, replica_groups=mesh['gx'=8,'gy'=4,'gz'=4] {'gx'}, use_global_device_ids=true, to_apply=%region_2.3 | all-reduce | flops 512 | bytes 4096 | tf_op jit(solution)/shard_map/psum | solution.py:137
  475.0 72.3 %all-reduce = (f32[16,16]{0,1:T(8,128)S(1)}, f32[16,16]{0,1:T(8,128)S(1)}) all-reduce(f32[16,16]{0,1:T(8,128)S(1)} %get-tuple-element.324, f32[16,16]{0,1:T(8,128)S(1)} %get-tuple-element.325), channel_id=1, replica_groups=mesh['gx'=8,'gy'=4,'gz'=4] {'gy','gz'}, use_global_device_ids=true, to_apply=%region_3.4 | all-reduce | flops 512 | bytes 4096 | tf_op jit(solution)/shard_map/psum | solution.py:137
  550.4 452.1 %while.35 = (s32[]{:T(128)}, f32[16,16]{1,0:T(8,128)S(1)}, f32[16,16]{0,1:T(8,128)S(1)}, s32[]{:T(128)}, s32[15,8]{1,0:T(8,128)}, /*index=5*/s32[]{:T(128)}, s32[]{:T(128)}, s32[15,8]{1,0:T(8,128)}) while((s32[]{:T(128)}, f32[16,16]{1,0:T(8,128)S(1)}, f32[16,16]{0,1:T(8,128)S(1)}, s32[]{:T(128)}, ...), condition=%wide.region_7.8_spmd.clone.clone, body=%wide.region_6.7_spmd.sunk.clone.clone.sunk | while | flops 249131 | bytes 19833 | solution.py:70
  (1624 shorter events, 639.3 us)
Async XLA Ops:
  1.5 5.5 collective-permute-start
  5.1 4.9 collective-permute-start.1
  12.9 5.2 collective-permute-start.3
  18.4 9.2 collective-permute-start.4
  20.0 8.0 collective-permute-start.5
  39.6 5.2 collective-permute-start.3
  45.1 9.2 collective-permute-start.4
  46.4 8.0 collective-permute-start.5
  59.2 4.9 collective-permute-start.1
  64.7 5.2 collective-permute-start.3
  70.2 9.2 collective-permute-start.4
  71.0 8.5 collective-permute-start.5
  84.1 4.9 collective-permute-start.1
  89.2 5.3 collective-permute-start.3
  94.7 9.8 collective-permute-start.4
  96.0 8.6 collective-permute-start.5
  109.2 4.9 collective-permute-start.1
  114.4 5.2 collective-permute-start.3
  119.9 10.4 %collective-permute-start.4 = (f32[20,36,2]{2,1,0:T(8,128)S(1)}, f32[20,36,2]{2,1,0:T(8,128)S(1)}, u32[]{:S(2)}, u32[]{:S(2)}) collective-permute-start(f32[20,36,2]{2,1,0:T(8,128)S(1)} %get-tuple-element.403), channel_id=1, source_target_pairs={{0,1},{1,2},{2,3},{3,0},{4,5},{5,6},{6,7},{7,4},{8,9},{9,10},{10,1... | collective-permute-start | bytes 17288 | tf_op jit(solution)/shard_map/while/body/eval_jaxpr/ppermute | solution.py:19
  121.3 9.0 collective-permute-start.5
  134.9 4.9 collective-permute-start.1
  140.2 5.2 collective-permute-start.3
  145.7 10.1 collective-permute-start.4
  147.0 8.7 collective-permute-start.5
  160.4 4.9 collective-permute-start.1
  165.6 5.2 collective-permute-start.3
  171.1 9.9 collective-permute-start.4
  172.5 8.5 collective-permute-start.5
  185.7 4.9 collective-permute-start.1
  191.1 5.2 collective-permute-start.3
  196.6 9.2 collective-permute-start.4
  197.9 8.0 collective-permute-start.5
  210.5 4.9 collective-permute-start.1
  215.6 5.2 collective-permute-start.3
  221.1 10.0 collective-permute-start.4
  222.8 8.3 collective-permute-start.5
  235.8 4.9 collective-permute-start.1
  241.0 5.2 collective-permute-start.3
  246.5 10.4 %collective-permute-start.4 = (f32[20,36,2]{2,1,0:T(8,128)S(1)}, f32[20,36,2]{2,1,0:T(8,128)S(1)}, u32[]{:S(2)}, u32[]{:S(2)}) collective-permute-start(f32[20,36,2]{2,1,0:T(8,128)S(1)} %get-tuple-element.403), channel_id=1, source_target_pairs={{0,1},{1,2},{2,3},{3,0},{4,5},{5,6},{6,7},{7,4},{8,9},{9,10},{10,1... | collective-permute-start | bytes 17288 | tf_op jit(solution)/shard_map/while/body/eval_jaxpr/ppermute | solution.py:19
  247.9 9.0 collective-permute-start.5
  261.5 4.9 collective-permute-start.1
  266.8 5.2 collective-permute-start.3
  272.3 9.9 collective-permute-start.4
  273.6 8.6 collective-permute-start.5
  286.9 4.9 collective-permute-start.1
  292.2 5.2 collective-permute-start.3
  297.7 9.2 collective-permute-start.4
  299.0 8.0 collective-permute-start.5
  311.7 4.9 collective-permute-start.1
  317.0 5.2 collective-permute-start.3
  322.5 9.8 collective-permute-start.4
  324.1 8.2 collective-permute-start.5
  337.0 4.9 collective-permute-start.1
  342.2 5.2 collective-permute-start.3
  347.7 10.4 %collective-permute-start.4 = (f32[20,36,2]{2,1,0:T(8,128)S(1)}, f32[20,36,2]{2,1,0:T(8,128)S(1)}, u32[]{:S(2)}, u32[]{:S(2)}) collective-permute-start(f32[20,36,2]{2,1,0:T(8,128)S(1)} %get-tuple-element.403), channel_id=1, source_target_pairs={{0,1},{1,2},{2,3},{3,0},{4,5},{5,6},{6,7},{7,4},{8,9},{9,10},{10,1... | collective-permute-start | bytes 17288 | tf_op jit(solution)/shard_map/while/body/eval_jaxpr/ppermute | solution.py:19
  349.1 9.0 collective-permute-start.5
  362.7 4.9 collective-permute-start.1
  368.0 5.2 collective-permute-start.3
  373.5 9.9 collective-permute-start.4
  374.8 8.6 collective-permute-start.5
  388.1 4.9 collective-permute-start.1
  393.4 5.2 collective-permute-start.3
  398.9 9.2 collective-permute-start.4
  400.2 8.0 collective-permute-start.5
  (33 other events, 126.2 us)
